TPU v7x, 32 devices: a whole 2x2x4 slice. The times are simulated.
32 devices in a mesh: groups: 2 (over x), ctx: 16 (over z, y, core).
Axes of the slice: x: 2, y: 2, z: 4, core: 2. Of those that a mesh axis runs over, the one named last changes fastest.
Arguments:
- queries: bfloat16 [2048, 4096], P(('groups', 'ctx')), parts along dimension 0, may hold values from -256 to 256
- text_keys: bfloat16 [2048, 512], P(('groups', 'ctx')), parts along dimension 0, may hold values from -4 to 4
- text_values: bfloat16 [2048, 512], P(('groups', 'ctx')), parts along dimension 0, may hold values from -5 to 5
- image_features: bfloat16 [16384, 256], P(('groups', 'ctx')), parts along dimension 0, may hold values from -300 to 300
- kv_weight: bfloat16 [8192, 1024], P('ctx'), may hold values from -0.0625 to 0.0625
- image_grids: int32 [32, 3], P(('groups', 'ctx')), parts along dimension 0, may hold values from 0 to 58, as said below
Outputs:
- attention: bfloat16 [2048, 4096], P(('groups', 'ctx')), parts along dimension 0
- cache_keys: bfloat16 [2048, 512], P(('groups', 'ctx')), parts along dimension 0
- cache_values: bfloat16 [2048, 512], P(('groups', 'ctx')), parts along dimension 0
There are 2 independent parts, one for each index of `groups`. A program takes and returns all parts, laid end to end along the dimension named above; an argument that names none is the same for every part. Nothing has to cross between parts.
Inputs may be any that keep to these rules, and one draw needn't show every extreme that they name: `image_grids`: row b describes the one image of context shard b: offset o, grid rows gh and grid columns gw with 2 <= gh, gw <= 4; its tokens take positions b * 64 + o to b * 64 + o + gh * gw - 1, token k at grid row k // gw and column k % gw; o + gh * gw <= 62; some shard has a 4 x 4 image.
All inputs are finite; a program needn't handle non-finite values.
Results may differ from a plain program's by a relative error of at most 0.0053.
Values may be sent and summed in bfloat16 or wider, within the bound.
No kernel may reach another device: no remote copies, remote signals or barrier semaphores. Data moves between devices by JAX's collectives and lax.ppermute only.
A program may use at most 128 MiB of HBM per device.

v0:
```python
import math
import jax
import jax.numpy as jnp
from jax import lax
from jax.sharding import PartitionSpec as P

D = 8192
HEAD_DIM = 128
GRID = 4


def rope_tables(time_ids, height_ids, width_ids):
    half_dim = HEAD_DIM // 2
    first_bound = HEAD_DIM // 8
    second_bound = first_bound + 3 * HEAD_DIM // 16
    pair_index = jnp.arange(half_dim, dtype=jnp.int32)
    inv_freq = 1000000.0 ** (-(2.0 * pair_index.astype(jnp.float32)) / HEAD_DIM)
    chosen = jnp.where(
        pair_index[None, :] < first_bound,
        time_ids[:, None],
        jnp.where(pair_index[None, :] < second_bound, height_ids[:, None], width_ids[:, None]),
    )
    angles = chosen.astype(jnp.float32) * inv_freq[None, :]
    cosine = jnp.concatenate([jnp.cos(angles), jnp.cos(angles)], axis=1)
    sine_table = jnp.concatenate([jnp.sin(angles), jnp.sin(angles)], axis=1)
    return (cosine, sine_table)


def rotate(key_heads, cosine, sine_table):
    half_dim = HEAD_DIM // 2
    turned = jnp.concatenate([-key_heads[..., half_dim:], key_heads[..., :half_dim]], axis=-1)
    return key_heads * cosine[:, None, :] + turned * sine_table[:, None, :]


def prepare(query_rows, kv_count, head_group):
    count_rows = query_rows.shape[0]
    shaped = query_rows.reshape(count_rows, kv_count, head_group, HEAD_DIM)
    return shaped.transpose(1, 2, 0, 3).reshape(kv_count, head_group * count_rows, HEAD_DIM)


def finish(summed, totals, count_rows, kv_count, head_group):
    blended = summed / totals[..., None]
    blended = blended.reshape(kv_count, head_group, count_rows, HEAD_DIM).transpose(2, 0, 1, 3)
    return blended.reshape(count_rows, kv_count * head_group * HEAD_DIM).astype(jnp.bfloat16)


def update(carry_state, query_set, positions, block_keys, block_values, key_start):
    running_max, running_sum, running_out = carry_state
    score_scale = 1.0 / math.sqrt(HEAD_DIM)
    scores = (
        jnp.einsum("grd,kgd->grk", query_set, block_keys, preferred_element_type=jnp.float32)
        * score_scale
    )
    key_pos = key_start + jnp.arange(block_keys.shape[0], dtype=jnp.int32)
    allowed = key_pos[None, None, :] <= positions[None, :, None]
    scores = jnp.where(allowed, scores, -1e30)
    new_max = jnp.maximum(running_max, jnp.max(scores, axis=-1))
    shrink = jnp.exp(running_max - new_max)
    weight = jnp.where(allowed, jnp.exp(scores - new_max[..., None]), 0.0)
    running_sum = running_sum * shrink + jnp.sum(weight, axis=-1)
    running_out = running_out * shrink[..., None] + jnp.einsum(
        "grk,kgd->grd",
        weight.astype(jnp.bfloat16),
        block_values,
        preferred_element_type=jnp.float32,
    )
    return (new_max, running_sum, running_out)


def body(queries, text_keys, text_values, image_features, kv_weight, image_grids):
    ctx_index = lax.axis_index("ctx")
    row_count = queries.shape[0]
    kv_width = text_keys.shape[1]
    kv_count = kv_width // HEAD_DIM
    head_group = queries.shape[1] // kv_width
    slot_count = GRID * GRID
    partial_kv = lax.dot_general(
        image_features, kv_weight, (((0,), (0,)), ((), ())), preferred_element_type=jnp.float32
    )
    feature_f32 = image_features.astype(jnp.float32)
    square_sums = jnp.sum(feature_f32 * feature_f32, axis=0)
    raw_kv, power_total = (
        lax.psum_scatter(partial_kv, "ctx", scatter_dimension=0, tiled=True),
        lax.psum_scatter(square_sums, "ctx", scatter_dimension=0, tiled=True),
    )
    normed = raw_kv * lax.rsqrt(power_total / D + 1e-06)[:, None]
    offset = image_grids[0, 0]
    grid_tall = image_grids[0, 1]
    grid_wide = image_grids[0, 2]
    within = jnp.arange(slot_count, dtype=jnp.int32)
    image_start = ctx_index * row_count + offset
    time_ids = jnp.broadcast_to(image_start, (slot_count,))
    height_ids = image_start + within // grid_wide
    width_ids = image_start + within % grid_wide
    cosine, sine_table = rope_tables(time_ids, height_ids, width_ids)
    key_heads = normed[:, :kv_width].reshape(slot_count, kv_count, HEAD_DIM)
    image_keys = (
        rotate(key_heads, cosine, sine_table).reshape(slot_count, kv_width).astype(jnp.bfloat16)
    )
    image_values = normed[:, kv_width:].astype(jnp.bfloat16)
    live_slot = within < grid_tall * grid_wide
    local_rows = jnp.arange(row_count, dtype=jnp.int32)
    one_hot = ((local_rows[:, None] == offset + within[None, :]) & live_slot[None, :]).astype(
        jnp.bfloat16
    )
    image_rows = (local_rows >= offset) & (local_rows < offset + grid_tall * grid_wide)
    placed = jnp.dot(
        one_hot,
        jnp.concatenate([image_keys, image_values], axis=1),
        preferred_element_type=jnp.float32,
    ).astype(jnp.bfloat16)
    cache_keys = jnp.where(image_rows[:, None], placed[:, :kv_width], text_keys)
    cache_values = jnp.where(image_rows[:, None], placed[:, kv_width:], text_values)
    half_rows = row_count // 2
    lead_queries = queries[:half_rows]
    trail_queries = queries[half_rows:]
    trail_base = ctx_index * row_count + half_rows
    lead_base = ctx_index * row_count
    query_sets = jnp.stack(
        [prepare(lead_queries, kv_count, head_group), prepare(trail_queries, kv_count, head_group)]
    )
    query_span = head_group * half_rows
    row_pos = jnp.arange(query_span, dtype=jnp.int32) % half_rows
    base_rows = jnp.stack([lead_base, trail_base])
    query_pos = base_rows[:, None] + row_pos[None, :]
    limits = base_rows + half_rows - 1
    initial = (
        jnp.full((2, kv_count, query_span), -1e30, jnp.float32),
        jnp.zeros((2, kv_count, query_span), jnp.float32),
        jnp.zeros((2, kv_count, query_span, HEAD_DIM), jnp.float32),
    )
    piece_keys = lax.all_gather(cache_keys, "ctx", axis=0, tiled=True)
    piece_values = lax.all_gather(cache_values, "ctx", axis=0, tiled=True)
    piece_size = piece_keys.shape[0]
    block_size = math.gcd(piece_size, 512)
    block_count = piece_size // block_size
    split_keys = piece_keys.reshape(block_count, block_size, kv_count, HEAD_DIM)
    split_values = piece_values.reshape(block_count, block_size, kv_count, HEAD_DIM)

    def scan_step(carried_state, scan_item):
        block_keys, block_values, number = scan_item
        key_start = number * block_size
        outcome = []
        for half_index in range(2):
            half_state = tuple((member[half_index] for member in carried_state))
            updated = lax.cond(
                key_start <= limits[half_index],
                lambda current: update(
                    current,
                    query_sets[half_index],
                    query_pos[half_index],
                    block_keys,
                    block_values,
                    key_start,
                ),
                lambda current: current,
                half_state,
            )
            outcome.append(updated)
        stacked = tuple(
            (
                jnp.stack([outcome[0][number_index], outcome[1][number_index]])
                for number_index in range(3)
            )
        )
        return (stacked, None)

    result_state, unused_out = lax.scan(
        scan_step, initial, (split_keys, split_values, jnp.arange(block_count, dtype=jnp.int32))
    )
    running_max, running_sum, running_out = result_state
    lead_out = finish(running_out[0], running_sum[0], half_rows, kv_count, head_group)
    trail_out = finish(running_out[1], running_sum[1], half_rows, kv_count, head_group)
    attention = jnp.concatenate([lead_out, trail_out], axis=0)
    return (attention, cache_keys, cache_values)


def solution(mesh):
    in_specs = (
        P(("groups", "ctx"), None),
        P(("groups", "ctx"), None),
        P(("groups", "ctx"), None),
        P(("groups", "ctx"), None),
        P("ctx", None),
        P(("groups", "ctx"), None),
    )
    out_specs = (P(("groups", "ctx"), None), P(("groups", "ctx"), None), P(("groups", "ctx"), None))
    return jax.shard_map(body, mesh=mesh, in_specs=in_specs, out_specs=out_specs, check_vma=False)
```

profile of v0, /device:TPU:25, one launch (start us, length us, event | category | flops | bytes accessed | tf_op | source)
XLA Modules:
  0.0 195.3 jit_solution(3191314341069254623)
XLA Ops:
  7.3 1.1 copy-done
  8.4 2.4 %fusion.47 = f32[256,1024]{1,0:T(8,128)} fusion(bf16[512,256]{1,0:T(8,128)(2,1)} %param.15, bf16[512,1024]{1,0:T(8,128)(2,1)S(1)} %copy-done), kind=kOutput, calls=%fused_computation.104 | convolution fusion | flops 268435456 | bytes 2359296 | tf_op jit(solution)/shard_map/dot_general | solution.py:77
  17.4 25.9 %all-reduce = f32[256]{0:T(256)S(1)} all-reduce(f32[256]{0:T(256)S(1)} %multiply_reduce_fusion), channel_id=3, replica_groups=mesh['groups'=2,'ctx'=16] {'ctx'}, use_global_device_ids=true, to_apply=%region_2.0.clone | all-reduce | flops 256 | bytes 2048
  43.3 0.7 iota_add_fusion.2
  44.0 0.7 compare_and_fusion
  44.7 0.8 fusion.39
  45.8 21.6 %reduce-scatter.2.cloned.1.call-done = f32[16,1024]{1,0:T(8,128)} async-done(((f32[256,1024]{1,0:T(8,128)}), f32[16,1024]{1,0:T(8,128)}) %reduce-scatter.2.cloned.1.call-update) | async-done | bytes 65552 | tf_op jit(solution)/shard_map/reduce_scatter | solution.py:83
  67.4 0.9 broadcast_multiply_fusion
  68.7 0.7 slice_select_fusion
  69.5 0.7 all-gather.5.cloned.1.call-update
  70.5 0.8 copy.26
  71.4 37.9 %all-gather.3.cloned.1.call-done = bf16[1024,512]{1,0:T(8,128)(2,1)} async-done(((bf16[64,512]{1,0:T(8,128)(2,1)}), bf16[1024,512]{1,0:T(8,128)(2,1)}) %all-gather.3.cloned.1.call-update) | async-done | bytes 1048592 | tf_op jit(solution)/shard_map/all_gather | solution.py:132
  109.3 2.2 %reshape.193 = bf16[2,512,4,128]{3,2,1,0:T(4,128)(2,1)} reshape(bf16[1024,512]{1,0:T(8,128)(2,1)} %all-gather.3.cloned.1.call-done) | data formatting | bytes 2097152 | tf_op jit(solution)/shard_map/reshape | solution.py:137
  111.4 37.4 %all-gather.5.cloned.1.call-done = bf16[1024,512]{1,0:T(8,128)(2,1)} async-done(((bf16[64,512]{1,0:T(8,128)(2,1)}), bf16[1024,512]{1,0:T(8,128)(2,1)}) %all-gather.5.cloned.1.call-update) | async-done | bytes 1048592 | tf_op jit(solution)/shard_map/all_gather | solution.py:133
  148.9 2.1 %reshape.194 = bf16[2,512,4,128]{3,2,1,0:T(4,128)(2,1)} reshape(bf16[1024,512]{1,0:T(8,128)(2,1)} %all-gather.5.cloned.1.call-done) | data formatting | bytes 2097152 | tf_op jit(solution)/shard_map/reshape | solution.py:138
  151.1 35.4 %while.15 = (s32[]{:T(128)}, f32[2,4,256]{2,1,0:T(4,128)S(1)}, f32[2,4,256]{2,1,0:T(4,128)S(1)}, f32[2,4,256,128]{3,2,1,0:T(8,128)S(1)}, s32[2]{0:T(128)S(1)}, /...) while((s32[]{:T(128)}, f32[2,4,256]{2,1,0:T(4,128)S(1)}, ...), condition=%wide.region_12.13_spmd.clone, body=%wide.region_3.12_spmd.clone.sunk | while | flops 551560704 | bytes 36390424 | solution.py:168
  151.1 0.7 dynamic_slice.19
  152.5 0.6 fusion.57
  153.8 0.6 slice_bitcast_fusion.10
  155.7 0.7 copy.87
  156.5 5.1 %conditional.6 = (f32[1,4,256]{2,1,0:T(4,128)}, f32[1,4,256]{2,1,0:T(4,128)S(1)}, f32[1,4,256,128]{3,2,1,0:T(8,128)S(1)}) conditional(s32[]{:T(128)} %convert_element_type.81, (f32[4,256]{1,0:T(4,128)}, f32[4,256]{1,0:T(4,128)S(1)}, f32[4,256,128]{2,1,0:T(8,128)S(1)}) %tuple.139, (s32[]{:T(128)}, s32[2,256]{1,0:T(2,128)S(1)}, ...), branch_computations={%region_8.8_spmd, %region_9.11_spmd} | conditional | flops 275646976 | bytes 9239580 | solution.py:146
  157.3 0.6 max.5
  157.8 1.5 fusion.16
  159.3 0.7 add_bitcast_fusion.1
  160.0 1.6 fusion.17
  162.3 0.7 copy.93
  162.9 5.1 %conditional.7 = (f32[1,4,256]{2,1,0:T(4,128)}, f32[1,4,256]{2,1,0:T(4,128)S(1)}, f32[1,4,256,128]{3,2,1,0:T(8,128)S(1)}) conditional(s32[]{:T(128)} %convert_element_type.82, (f32[4,256]{1,0:T(4,128)}, f32[4,256]{1,0:T(4,128)S(1)}, f32[4,256,128]{2,1,0:T(8,128)S(1)}) %tuple.141, (s32[]{:T(128)}, s32[2,256]{1,0:T(2,128)S(1)}, ...), branch_computations={%region_4.4_spmd, %region_5.7_spmd} | conditional | flops 275646976 | bytes 9239580 | solution.py:146
  163.7 0.6 max.4
  164.3 1.5 fusion.4
  165.7 0.7 add_bitcast_fusion
  166.4 1.6 fusion.5
  168.0 0.7 pad_maximum_fusion.9
  168.8 0.7 dynamic_slice.19
  170.2 0.6 fusion.57
  171.5 0.6 slice_bitcast_fusion.10
  173.4 0.7 copy.87
  174.2 5.1 %conditional.6 = (f32[1,4,256]{2,1,0:T(4,128)}, f32[1,4,256]{2,1,0:T(4,128)S(1)}, f32[1,4,256,128]{3,2,1,0:T(8,128)S(1)}) conditional(s32[]{:T(128)} %convert_element_type.81, (f32[4,256]{1,0:T(4,128)}, f32[4,256]{1,0:T(4,128)S(1)}, f32[4,256,128]{2,1,0:T(8,128)S(1)}) %tuple.139, (s32[]{:T(128)}, s32[2,256]{1,0:T(2,128)S(1)}, ...), branch_computations={%region_8.8_spmd, %region_9.11_spmd} | conditional | flops 275646976 | bytes 9239580 | solution.py:146
  175.5 1.5 fusion.16
  177.0 0.7 add_bitcast_fusion.1
  177.7 1.6 fusion.17
  179.9 0.7 copy.93
  180.6 5.1 %conditional.7 = (f32[1,4,256]{2,1,0:T(4,128)}, f32[1,4,256]{2,1,0:T(4,128)S(1)}, f32[1,4,256,128]{3,2,1,0:T(8,128)S(1)}) conditional(s32[]{:T(128)} %convert_element_type.82, (f32[4,256]{1,0:T(4,128)}, f32[4,256]{1,0:T(4,128)S(1)}, f32[4,256,128]{2,1,0:T(8,128)S(1)}) %tuple.141, (s32[]{:T(128)}, s32[2,256]{1,0:T(2,128)S(1)}, ...), branch_computations={%region_4.4_spmd, %region_5.7_spmd} | conditional | flops 275646976 | bytes 9239580 | solution.py:146
  181.4 0.6 max.4
  182.0 1.5 fusion.4
  183.4 0.7 add_bitcast_fusion
  184.1 1.6 fusion.5
  185.7 0.7 pad_maximum_fusion.9
  187.9 0.8 pad_maximum_fusion.3
  (99 shorter events, 10.5 us)
Async XLA Ops:
  7.2 1.2 copy-start
  7.2 8.9 %copy-start.9 = (u32[32]{0:T(128)S(1)}, u32[32]{0:T(128)}, u32[]{:S(2)}) copy-start(u32[32]{0:T(128)} %constant.92) | copy-start | bytes 388
  7.2 10.1 %copy-start.4 = (bf16[512,256]{1,0:T(8,128)(2,1)S(1)}, bf16[512,256]{1,0:T(8,128)(2,1)}, u32[]{:S(2)}) copy-start(bf16[512,256]{1,0:T(8,128)(2,1)} %param.15) | copy-start | bytes 786436
  7.2 3.7 %copy-start.8 = (s32[1,3]{1,0:T(1,128)S(1)}, s32[1,3]{1,0:T(1,128)}, u32[]{:S(2)}) copy-start(s32[1,3]{1,0:T(1,128)} %param.17) | copy-start | bytes 40
  7.2 61.5 %copy-start.6 = (bf16[64,512]{1,0:T(8,128)(2,1)S(1)}, bf16[64,512]{1,0:T(8,128)(2,1)}, u32[]{:S(2)}) copy-start(bf16[64,512]{1,0:T(8,128)(2,1)} %param.14) | copy-start | bytes 196612
  7.2 61.5 %copy-start.7 = (bf16[64,512]{1,0:T(8,128)(2,1)S(1)}, bf16[64,512]{1,0:T(8,128)(2,1)}, u32[]{:S(2)}) copy-start(bf16[64,512]{1,0:T(8,128)(2,1)} %param.13) | copy-start | bytes 196612
  7.2 63.0 %copy-start.5 = (bf16[64,4096]{1,0:T(8,128)(2,1)S(1)}, bf16[64,4096]{1,0:T(8,128)(2,1)}, u32[]{:S(2)}) copy-start(bf16[64,4096]{1,0:T(8,128)(2,1)} %param.12) | copy-start | bytes 1572868
  7.2 60.1 %reduce-scatter.2.cloned.1.call-start = ((), (), s32[]{:S(2)}) async-start(), calls=%async_computation.1 | async-start | bytes 1114112 | tf_op jit(solution)/shard_map/reduce_scatter | solution.py:83
  10.8 98.4 %all-gather.3.cloned.1.call-start = ((), (), s32[]{:S(2)}) async-start(), calls=%async_computation.2 | async-start | bytes 1114112 | tf_op jit(solution)/shard_map/all_gather | solution.py:132
  69.5 79.4 %all-gather.5.cloned.1.call-start = ((), (), s32[]{:S(2)}) async-start(), calls=%async_computation.3 | async-start | bytes 1114112 | tf_op jit(solution)/shard_map/all_gather | solution.py:133
  153.7 1.2 copy-start.1
  153.8 1.5 copy-start.2
  155.3 1.2 copy-start.3
  171.4 1.2 copy-start.1
  171.4 1.5 copy-start.2
  173.0 1.2 copy-start.3
Sparse Core Ops, SparseCore 0:
  11.7 55.6 reduce-scatter.1
  70.1 39.1 all-gather.2
  112.0 36.8 all-gather.4
where the time goes:
time: 196 us; the launch traced here: 195 us
  waiting for transfers between devices  97.6 us (50%)
  blocking collectives  25.9 us (13%)
  other arithmetic  19.3 us (10%)
  between operations  19.2 us (10%)
  local copies, waits for them, and re-layouts  17.6 us (9%)
  matrix products  11.3 us (6%)
  loops' own time  4.18 us (2%)
    all_gather x1, waiting for transfers between devices, body(): piece_keys = lax.all_gather(cache_keys, 'ctx', axis=0, tiled=True)  37.9 us
    all_gather x1, waiting for transfers between devices, body(): piece_values = lax.all_gather(cache_values, 'ctx', axis=0, tiled=True)  37.4 us
    unnamed x1, blocking collectives  25.9 us
    reduce_scatter x1, waiting for transfers between devices, body(): lax.psum_scatter(partial_kv, 'ctx', scatter_dimension=0, tiled=True)  21.6 us
    dot_general x4, matrix products, update(): jnp.einsum('grk,kgd->grd', weight.astype(jnp.bfloat16), block_values, pre...  6.43 us
    reduce_sum x4, other arithmetic, update(): running_sum = running_sum * shrink + jnp.sum(weight, axis=-1)  5.93 us
    while x16, local copies, waits for them, and re-layouts  4.29 us
    another operation x10, other arithmetic, scan_step(): jnp.stack([outcome[0][number_index], outcome[1][number_index]])  4.27 us
  transfers between devices with their start and end apart: 3, of which 3 were waited for; matrix products, arithmetic and copies ran while one was open for 4% of the time, Pallas kernels for 0%

commit v1 on v0

--- a/solution.py
+++ b/solution.py
@@ -129,7 +129,12 @@
         jnp.zeros((2, kv_count, query_span), jnp.float32),
         jnp.zeros((2, kv_count, query_span, HEAD_DIM), jnp.float32),
     )
-    piece_keys = lax.all_gather(cache_keys, "ctx", axis=0, tiled=True)
+    ring = [cache_keys]
+    for hop in range(15):
+        ring.append(lax.ppermute(ring[-1], "ctx", [(dev, (dev + 1) % 16) for dev in range(16)]))
+    piece_keys = jnp.roll(
+        jnp.concatenate(ring[::-1], axis=0), (lax.axis_index("ctx") + 1) * ring[0].shape[0], axis=0
+    )
     piece_values = lax.all_gather(cache_values, "ctx", axis=0, tiled=True)
     piece_size = piece_keys.shape[0]
     block_size = math.gcd(piece_size, 512)

time: 196 us -> 248 us (1.27)
  starting transfers between devices: 0.12 us -> 62.3 us
  waiting for transfers between devices: 97.6 us -> 87.5 us
    ppermute x0 -> x15, starting transfers between devices: none -> 62.2 us  [body(): lax.ppermute(ring[-1], 'ctx', [(dev, (dev + 1) % 16) for dev in range(16)])]
    all_gather x1 -> x0, waiting for transfers between devices: 37.9 us -> none  [body(): piece_keys = lax.all_gather(cache_keys, 'ctx', axis=0, tiled=True)]
    ppermute x0 -> x15, waiting for transfers between devices: none -> 22.1 us  [body(): lax.ppermute(ring[-1], 'ctx', [(dev, (dev + 1) % 16) for dev in range(16)])]
    all_gather x1, waiting for transfers between devices: 37.4 us -> 43.8 us  [body(): piece_values = lax.all_gather(cache_values, 'ctx', axis=0, tiled=True)]
  transfers between devices with their start and end apart: 3 -> 17, of which waited for: 3 -> 17; matrix products, arithmetic and copies ran while one was open for 4% -> 3% of each run, Pallas kernels for 0% -> 0%
where the time goes in v1:
time: 248 us; the launch traced here: 247 us
  waiting for transfers between devices  87.5 us (35%)
  starting transfers between devices  62.3 us (25%)
  blocking collectives  25.9 us (10%)
  between operations  19.8 us (8%)
  other arithmetic  19.4 us (8%)
  local copies, waits for them, and re-layouts  16.8 us (7%)
  matrix products  11.4 us (5%)
  loops' own time  4.22 us (2%)
    ppermute x15, starting transfers between devices, body(): lax.ppermute(ring[-1], 'ctx', [(dev, (dev + 1) % 16) for dev in range(16)])  62.2 us
    all_gather x1, waiting for transfers between devices, body(): piece_values = lax.all_gather(cache_values, 'ctx', axis=0, tiled=True)  43.8 us
    unnamed x1, blocking collectives  25.9 us
    ppermute x15, waiting for transfers between devices, body(): lax.ppermute(ring[-1], 'ctx', [(dev, (dev + 1) % 16) for dev in range(16)])  22.1 us
    reduce_scatter x1, waiting for transfers between devices, body(): lax.psum_scatter(partial_kv, 'ctx', scatter_dimension=0, tiled=True)  21.6 us
    dot_general x4, matrix products, update(): jnp.einsum('grk,kgd->grd', weight.astype(jnp.bfloat16), block_values, pre...  6.58 us
    reduce_sum x4, other arithmetic, update(): running_sum = running_sum * shrink + jnp.sum(weight, axis=-1)  5.98 us
  transfers between devices with their start and end apart: 17, of which 17 were waited for; matrix products, arithmetic and copies ran while one was open for 3% of the time, Pallas kernels for 0%

profile of v1, /device:TPU:25, one launch (start us, length us, event | category | flops | bytes accessed | tf_op | source)
XLA Modules:
  0.0 247.4 jit_solution(10676101617557000118)
XLA Ops:
  7.3 1.1 copy-done
  8.4 2.4 fusion.47
  17.4 25.9 %all-reduce = f32[256]{0:T(256)S(1)} all-reduce(f32[256]{0:T(256)S(1)} %multiply_reduce_fusion), channel_id=3, replica_groups=mesh['groups'=2,'ctx'=16] {'ctx'}, use_global_device_ids=true, to_apply=%region_2.0.clone | all-reduce | flops 256 | bytes 2048
  45.8 21.6 %reduce-scatter.2.cloned.1.call-done = f32[16,1024]{1,0:T(8,128)} async-done(((f32[256,1024]{1,0:T(8,128)}), f32[16,1024]{1,0:T(8,128)}) %reduce-scatter.2.cloned.1.call-update) | async-done | bytes 65552 | tf_op jit(solution)/shard_map/reduce_scatter | solution.py:83
  69.4 2.7 %collective-permute-start = (bf16[64,512]{1,0:T(8,128)(2,1)S(1)}, bf16[64,512]{1,0:T(8,128)(2,1)S(1)}, u32[]{:S(2)}, u32[]{:S(2)}) collective-permute-start(bf16[64,512]{1,0:T(8,128)(2,1)S(1)} %get-tuple-element.298), channel_id=1, source_target_pairs={{0,1},{1,2},{2,3},{3,4},{4,5},{5,6},{6,7},{7,8},{8,9},{9,10},{10,1... | collective-permute-start | bytes 196616 | tf_op jit(solution)/shard_map/ppermute | solution.py:134
  72.1 1.3 collective-permute-done
  73.5 2.4 collective-permute-start.1
  75.8 1.5 collective-permute-done.1
  77.3 2.2 collective-permute-start.2
  79.5 2.4 collective-permute-done.2
  81.9 1.3 collective-permute-start.3
  83.3 3.2 %collective-permute-done.3 = bf16[64,512]{1,0:T(8,128)(2,1)S(1)} collective-permute-done((bf16[64,512]{1,0:T(8,128)(2,1)S(1)}, bf16[64,512]{1,0:T(8,128)(2,1)S(1)}, u32[]{:S(2)}, u32[]{:S(2)}) %collective-permute-start.3) | collective-permute-done | bytes 65568 | tf_op jit(solution)/shard_map/ppermute | solution.py:134
  86.5 3.1 %collective-permute-start.4 = (bf16[64,512]{1,0:T(8,128)(2,1)S(1)}, bf16[64,512]{1,0:T(8,128)(2,1)S(1)}, u32[]{:S(2)}, u32[]{:S(2)}) collective-permute-start(bf16[64,512]{1,0:T(8,128)(2,1)S(1)} %collective-permute-done.3), channel_id=1, source_target_pairs={{0,1},{1,2},{2,3},{3,4},{4,5},{5,6},{6,7},{7,8},{8,9},{9,10},{10,1... | collective-permute-start | bytes 196616 | tf_op jit(solution)/shard_map/ppermute | solution.py:134
  89.7 1.4 collective-permute-done.4
  91.1 4.9 %collective-permute-start.5 = (bf16[64,512]{1,0:T(8,128)(2,1)S(1)}, bf16[64,512]{1,0:T(8,128)(2,1)S(1)}, u32[]{:S(2)}, u32[]{:S(2)}) collective-permute-start(bf16[64,512]{1,0:T(8,128)(2,1)S(1)} %collective-permute-done.4), channel_id=1, source_target_pairs={{0,1},{1,2},{2,3},{3,4},{4,5},{5,6},{6,7},{7,8},{8,9},{9,10},{10,1... | collective-permute-start | bytes 196616 | tf_op jit(solution)/shard_map/ppermute | solution.py:134
  96.1 1.3 collective-permute-done.5
  97.4 5.1 %collective-permute-start.6 = (bf16[64,512]{1,0:T(8,128)(2,1)S(1)}, bf16[64,512]{1,0:T(8,128)(2,1)S(1)}, u32[]{:S(2)}, u32[]{:S(2)}) collective-permute-start(bf16[64,512]{1,0:T(8,128)(2,1)S(1)} %collective-permute-done.5), channel_id=1, source_target_pairs={{0,1},{1,2},{2,3},{3,4},{4,5},{5,6},{6,7},{7,8},{8,9},{9,10},{10,1... | collective-permute-start | bytes 196616 | tf_op jit(solution)/shard_map/ppermute | solution.py:134
  102.4 1.3 collective-permute-done.6
  103.8 5.1 %collective-permute-start.7 = (bf16[64,512]{1,0:T(8,128)(2,1)S(1)}, bf16[64,512]{1,0:T(8,128)(2,1)S(1)}, u32[]{:S(2)}, u32[]{:S(2)}) collective-permute-start(bf16[64,512]{1,0:T(8,128)(2,1)S(1)} %collective-permute-done.6), channel_id=1, source_target_pairs={{0,1},{1,2},{2,3},{3,4},{4,5},{5,6},{6,7},{7,8},{8,9},{9,10},{10,1... | collective-permute-start | bytes 196616 | tf_op jit(solution)/shard_map/ppermute | solution.py:134
  108.8 1.3 collective-permute-done.7
  110.2 5.1 %collective-permute-start.8 = (bf16[64,512]{1,0:T(8,128)(2,1)S(1)}, bf16[64,512]{1,0:T(8,128)(2,1)S(1)}, u32[]{:S(2)}, u32[]{:S(2)}) collective-permute-start(bf16[64,512]{1,0:T(8,128)(2,1)S(1)} %collective-permute-done.7), channel_id=1, source_target_pairs={{0,1},{1,2},{2,3},{3,4},{4,5},{5,6},{6,7},{7,8},{8,9},{9,10},{10,1... | collective-permute-start | bytes 196616 | tf_op jit(solution)/shard_map/ppermute | solution.py:134
  115.2 1.3 collective-permute-done.8
  116.6 5.1 %collective-permute-start.9 = (bf16[64,512]{1,0:T(8,128)(2,1)S(1)}, bf16[64,512]{1,0:T(8,128)(2,1)S(1)}, u32[]{:S(2)}, u32[]{:S(2)}) collective-permute-start(bf16[64,512]{1,0:T(8,128)(2,1)S(1)} %collective-permute-done.8), channel_id=1, source_target_pairs={{0,1},{1,2},{2,3},{3,4},{4,5},{5,6},{6,7},{7,8},{8,9},{9,10},{10,1... | collective-permute-start | bytes 196616 | tf_op jit(solution)/shard_map/ppermute | solution.py:134
  121.6 1.3 collective-permute-done.9
  122.9 5.1 %collective-permute-start.10 = (bf16[64,512]{1,0:T(8,128)(2,1)S(1)}, bf16[64,512]{1,0:T(8,128)(2,1)S(1)}, u32[]{:S(2)}, u32[]{:S(2)}) collective-permute-start(bf16[64,512]{1,0:T(8,128)(2,1)S(1)} %collective-permute-done.9), channel_id=1, source_target_pairs={{0,1},{1,2},{2,3},{3,4},{4,5},{5,6},{6,7},{7,8},{8,9},{9,10},{10,1... | collective-permute-start | bytes 196616 | tf_op jit(solution)/shard_map/ppermute | solution.py:134
  128.0 1.3 collective-permute-done.10
  129.3 5.1 %collective-permute-start.11 = (bf16[64,512]{1,0:T(8,128)(2,1)S(1)}, bf16[64,512]{1,0:T(8,128)(2,1)S(1)}, u32[]{:S(2)}, u32[]{:S(2)}) collective-permute-start(bf16[64,512]{1,0:T(8,128)(2,1)S(1)} %collective-permute-done.10), channel_id=1, source_target_pairs={{0,1},{1,2},{2,3},{3,4},{4,5},{5,6},{6,7},{7,8},{8,9},{9,10},{10,1... | collective-permute-start | bytes 196616 | tf_op jit(solution)/shard_map/ppermute | solution.py:134
  134.4 1.3 collective-permute-done.11
  135.7 5.1 %collective-permute-start.12 = (bf16[64,512]{1,0:T(8,128)(2,1)S(1)}, bf16[64,512]{1,0:T(8,128)(2,1)S(1)}, u32[]{:S(2)}, u32[]{:S(2)}) collective-permute-start(bf16[64,512]{1,0:T(8,128)(2,1)S(1)} %collective-permute-done.11), channel_id=1, source_target_pairs={{0,1},{1,2},{2,3},{3,4},{4,5},{5,6},{6,7},{7,8},{8,9},{9,10},{10,1... | collective-permute-start | bytes 196616 | tf_op jit(solution)/shard_map/ppermute | solution.py:134
  142.1 5.2 %collective-permute-start.13 = (bf16[64,512]{1,0:T(8,128)(2,1)S(1)}, bf16[64,512]{1,0:T(8,128)(2,1)S(1)}, u32[]{:S(2)}, u32[]{:S(2)}) collective-permute-start(bf16[64,512]{1,0:T(8,128)(2,1)S(1)} %collective-permute-done.12), channel_id=1, source_target_pairs={{0,1},{1,2},{2,3},{3,4},{4,5},{5,6},{6,7},{7,8},{8,9},{9,10},{10,1... | collective-permute-start | bytes 196616 | tf_op jit(solution)/shard_map/ppermute | solution.py:134
  147.3 1.3 collective-permute-done.13
  148.7 4.9 %collective-permute-start.14 = (bf16[64,512]{1,0:T(8,128)(2,1)S(1)}, bf16[64,512]{1,0:T(8,128)(2,1)S(1)}, u32[]{:S(2)}, u32[]{:S(2)}) collective-permute-start(bf16[64,512]{1,0:T(8,128)(2,1)S(1)} %collective-permute-done.13), channel_id=1, source_target_pairs={{0,1},{1,2},{2,3},{3,4},{4,5},{5,6},{6,7},{7,8},{8,9},{9,10},{10,1... | collective-permute-start | bytes 196616 | tf_op jit(solution)/shard_map/ppermute | solution.py:134
  153.7 1.2 collective-permute-done.14
  156.6 43.8 %all-gather.2.cloned.1.call-done = bf16[1024,512]{1,0:T(8,128)(2,1)} async-done(((bf16[64,512]{1,0:T(8,128)(2,1)}), bf16[1024,512]{1,0:T(8,128)(2,1)}) %all-gather.2.cloned.1.call-update) | async-done | bytes 1048592 | tf_op jit(solution)/shard_map/all_gather | solution.py:138
  200.4 2.1 reshape.194
  202.6 35.8 %while.15 = (s32[]{:T(128)}, f32[2,4,256]{2,1,0:T(4,128)S(1)}, f32[2,4,256]{2,1,0:T(4,128)S(1)}, f32[2,4,256,128]{3,2,1,0:T(8,128)S(1)}, s32[2]{0:T(128)S(1)}, /...) while((s32[]{:T(128)}, f32[2,4,256]{2,1,0:T(4,128)S(1)}, ...), condition=%wide.region_12.13_spmd.clone, body=%wide.region_3.12_spmd.clone.sunk | while | flops 551560704 | bytes 36390424 | solution.py:173
  207.9 5.2 %conditional.6 = (f32[1,4,256]{2,1,0:T(4,128)}, f32[1,4,256]{2,1,0:T(4,128)S(1)}, f32[1,4,256,128]{3,2,1,0:T(8,128)S(1)}) conditional(s32[]{:T(128)} %convert_element_type.81, (f32[4,256]{1,0:T(4,128)}, f32[4,256]{1,0:T(4,128)S(1)}, f32[4,256,128]{2,1,0:T(8,128)S(1)}) %tuple.139, (s32[]{:T(128)}, s32[2,256]{1,0:T(2,128)S(1)}, ...), branch_computations={%region_8.8_spmd, %region_9.11_spmd} | conditional | flops 275646976 | bytes 9239580 | solution.py:151
  209.3 1.5 fusion.16
  211.5 1.6 fusion.17
  214.5 5.2 %conditional.7 = (f32[1,4,256]{2,1,0:T(4,128)}, f32[1,4,256]{2,1,0:T(4,128)S(1)}, f32[1,4,256,128]{3,2,1,0:T(8,128)S(1)}) conditional(s32[]{:T(128)} %convert_element_type.82, (f32[4,256]{1,0:T(4,128)}, f32[4,256]{1,0:T(4,128)S(1)}, f32[4,256,128]{2,1,0:T(8,128)S(1)}) %tuple.141, (s32[]{:T(128)}, s32[2,256]{1,0:T(2,128)S(1)}, ...), branch_computations={%region_4.4_spmd, %region_5.7_spmd} | conditional | flops 275646976 | bytes 9239580 | solution.py:151
  215.9 1.5 fusion.4
  218.0 1.6 fusion.5
  225.8 5.2 %conditional.6 = (f32[1,4,256]{2,1,0:T(4,128)}, f32[1,4,256]{2,1,0:T(4,128)S(1)}, f32[1,4,256,128]{3,2,1,0:T(8,128)S(1)}) conditional(s32[]{:T(128)} %convert_element_type.81, (f32[4,256]{1,0:T(4,128)}, f32[4,256]{1,0:T(4,128)S(1)}, f32[4,256,128]{2,1,0:T(8,128)S(1)}) %tuple.139, (s32[]{:T(128)}, s32[2,256]{1,0:T(2,128)S(1)}, ...), branch_computations={%region_8.8_spmd, %region_9.11_spmd} | conditional | flops 275646976 | bytes 9239580 | solution.py:151
  227.2 1.5 fusion.16
  229.4 1.6 fusion.17
  232.4 5.2 %conditional.7 = (f32[1,4,256]{2,1,0:T(4,128)}, f32[1,4,256]{2,1,0:T(4,128)S(1)}, f32[1,4,256,128]{3,2,1,0:T(8,128)S(1)}) conditional(s32[]{:T(128)} %convert_element_type.82, (f32[4,256]{1,0:T(4,128)}, f32[4,256]{1,0:T(4,128)S(1)}, f32[4,256,128]{2,1,0:T(8,128)S(1)}) %tuple.141, (s32[]{:T(128)}, s32[2,256]{1,0:T(2,128)S(1)}, ...), branch_computations={%region_4.4_spmd, %region_5.7_spmd} | conditional | flops 275646976 | bytes 9239580 | solution.py:151
  233.7 1.5 fusion.4
  235.9 1.6 fusion.5
  (161 shorter events, 29.9 us)
Async XLA Ops:
  7.2 1.2 copy-start
  7.2 8.8 %copy-start.10 = (u32[32]{0:T(128)S(1)}, u32[32]{0:T(128)}, u32[]{:S(2)}) copy-start(u32[32]{0:T(128)} %constant.114) | copy-start | bytes 388
  7.2 10.1 %copy-start.4 = (bf16[512,256]{1,0:T(8,128)(2,1)S(1)}, bf16[512,256]{1,0:T(8,128)(2,1)}, u32[]{:S(2)}) copy-start(bf16[512,256]{1,0:T(8,128)(2,1)} %param.15) | copy-start | bytes 786436
  7.2 3.7 %copy-start.9 = (s32[1,3]{1,0:T(1,128)S(1)}, s32[1,3]{1,0:T(1,128)}, u32[]{:S(2)}) copy-start(s32[1,3]{1,0:T(1,128)} %param.17) | copy-start | bytes 40
  7.2 61.5 %copy-start.7 = (bf16[64,512]{1,0:T(8,128)(2,1)S(1)}, bf16[64,512]{1,0:T(8,128)(2,1)}, u32[]{:S(2)}) copy-start(bf16[64,512]{1,0:T(8,128)(2,1)} %param.14) | copy-start | bytes 196612
  7.2 61.5 %copy-start.8 = (bf16[64,512]{1,0:T(8,128)(2,1)S(1)}, bf16[64,512]{1,0:T(8,128)(2,1)}, u32[]{:S(2)}) copy-start(bf16[64,512]{1,0:T(8,128)(2,1)} %param.13) | copy-start | bytes 196612
  7.2 133.5 %copy-start.6 = (bf16[64,4096]{1,0:T(8,128)(2,1)S(1)}, bf16[64,4096]{1,0:T(8,128)(2,1)}, u32[]{:S(2)}) copy-start(bf16[64,4096]{1,0:T(8,128)(2,1)} %param.12) | copy-start | bytes 1572868
  7.2 60.1 %reduce-scatter.2.cloned.1.call-start = ((), (), s32[]{:S(2)}) async-start(), calls=%async_computation.1 | async-start | bytes 1114112 | tf_op jit(solution)/shard_map/reduce_scatter | solution.py:83
  10.8 189.6 %all-gather.2.cloned.1.call-start = ((), (), s32[]{:S(2)}) async-start(), calls=%async_computation.2 | async-start | bytes 1114112 | tf_op jit(solution)/shard_map/all_gather | solution.py:138
  69.4 85.9 %copy-start.5 = (bf16[64,512]{1,0:T(8,128)(2,1)}, bf16[64,512]{1,0:T(8,128)(2,1)S(1)}, u32[]{:S(2)}) copy-start(bf16[64,512]{1,0:T(8,128)(2,1)S(1)} %get-tuple-element.298) | copy-start | bytes 196612
  69.4 4.1 %collective-permute-start = (bf16[64,512]{1,0:T(8,128)(2,1)S(1)}, bf16[64,512]{1,0:T(8,128)(2,1)S(1)}, u32[]{:S(2)}, u32[]{:S(2)}) collective-permute-start(bf16[64,512]{1,0:T(8,128)(2,1)S(1)} %get-tuple-element.298), channel_id=1, source_target_pairs={{0,1},{1,2},{2,3},{3,4},{4,5},{5,6},{6,7},{7,8},{8,9},{9,10},{10,1... | collective-permute-start | bytes 196616 | tf_op jit(solution)/shard_map/ppermute | solution.py:134
  73.5 3.9 %collective-permute-start.1 = (bf16[64,512]{1,0:T(8,128)(2,1)S(1)}, bf16[64,512]{1,0:T(8,128)(2,1)S(1)}, u32[]{:S(2)}, u32[]{:S(2)}) collective-permute-start(bf16[64,512]{1,0:T(8,128)(2,1)S(1)} %collective-permute-done), channel_id=1, source_target_pairs={{0,1},{1,2},{2,3},{3,4},{4,5},{5,6},{6,7},{7,8},{8,9},{9,10},{10,1... | collective-permute-start | bytes 196616 | tf_op jit(solution)/shard_map/ppermute | solution.py:134
  77.3 4.6 %collective-permute-start.2 = (bf16[64,512]{1,0:T(8,128)(2,1)S(1)}, bf16[64,512]{1,0:T(8,128)(2,1)S(1)}, u32[]{:S(2)}, u32[]{:S(2)}) collective-permute-start(bf16[64,512]{1,0:T(8,128)(2,1)S(1)} %collective-permute-done.1), channel_id=1, source_target_pairs={{0,1},{1,2},{2,3},{3,4},{4,5},{5,6},{6,7},{7,8},{8,9},{9,10},{10,1... | collective-permute-start | bytes 196616 | tf_op jit(solution)/shard_map/ppermute | solution.py:134
  81.9 4.6 %collective-permute-start.3 = (bf16[64,512]{1,0:T(8,128)(2,1)S(1)}, bf16[64,512]{1,0:T(8,128)(2,1)S(1)}, u32[]{:S(2)}, u32[]{:S(2)}) collective-permute-start(bf16[64,512]{1,0:T(8,128)(2,1)S(1)} %collective-permute-done.2), channel_id=1, source_target_pairs={{0,1},{1,2},{2,3},{3,4},{4,5},{5,6},{6,7},{7,8},{8,9},{9,10},{10,1... | collective-permute-start | bytes 196616 | tf_op jit(solution)/shard_map/ppermute | solution.py:134
  86.5 4.6 %collective-permute-start.4 = (bf16[64,512]{1,0:T(8,128)(2,1)S(1)}, bf16[64,512]{1,0:T(8,128)(2,1)S(1)}, u32[]{:S(2)}, u32[]{:S(2)}) collective-permute-start(bf16[64,512]{1,0:T(8,128)(2,1)S(1)} %collective-permute-done.3), channel_id=1, source_target_pairs={{0,1},{1,2},{2,3},{3,4},{4,5},{5,6},{6,7},{7,8},{8,9},{9,10},{10,1... | collective-permute-start | bytes 196616 | tf_op jit(solution)/shard_map/ppermute | solution.py:134
  91.1 6.3 %collective-permute-start.5 = (bf16[64,512]{1,0:T(8,128)(2,1)S(1)}, bf16[64,512]{1,0:T(8,128)(2,1)S(1)}, u32[]{:S(2)}, u32[]{:S(2)}) collective-permute-start(bf16[64,512]{1,0:T(8,128)(2,1)S(1)} %collective-permute-done.4), channel_id=1, source_target_pairs={{0,1},{1,2},{2,3},{3,4},{4,5},{5,6},{6,7},{7,8},{8,9},{9,10},{10,1... | collective-permute-start | bytes 196616 | tf_op jit(solution)/shard_map/ppermute | solution.py:134
  97.4 6.4 %collective-permute-start.6 = (bf16[64,512]{1,0:T(8,128)(2,1)S(1)}, bf16[64,512]{1,0:T(8,128)(2,1)S(1)}, u32[]{:S(2)}, u32[]{:S(2)}) collective-permute-start(bf16[64,512]{1,0:T(8,128)(2,1)S(1)} %collective-permute-done.5), channel_id=1, source_target_pairs={{0,1},{1,2},{2,3},{3,4},{4,5},{5,6},{6,7},{7,8},{8,9},{9,10},{10,1... | collective-permute-start | bytes 196616 | tf_op jit(solution)/shard_map/ppermute | solution.py:134
  103.8 6.4 %collective-permute-start.7 = (bf16[64,512]{1,0:T(8,128)(2,1)S(1)}, bf16[64,512]{1,0:T(8,128)(2,1)S(1)}, u32[]{:S(2)}, u32[]{:S(2)}) collective-permute-start(bf16[64,512]{1,0:T(8,128)(2,1)S(1)} %collective-permute-done.6), channel_id=1, source_target_pairs={{0,1},{1,2},{2,3},{3,4},{4,5},{5,6},{6,7},{7,8},{8,9},{9,10},{10,1... | collective-permute-start | bytes 196616 | tf_op jit(solution)/shard_map/ppermute | solution.py:134
  110.2 6.4 %collective-permute-start.8 = (bf16[64,512]{1,0:T(8,128)(2,1)S(1)}, bf16[64,512]{1,0:T(8,128)(2,1)S(1)}, u32[]{:S(2)}, u32[]{:S(2)}) collective-permute-start(bf16[64,512]{1,0:T(8,128)(2,1)S(1)} %collective-permute-done.7), channel_id=1, source_target_pairs={{0,1},{1,2},{2,3},{3,4},{4,5},{5,6},{6,7},{7,8},{8,9},{9,10},{10,1... | collective-permute-start | bytes 196616 | tf_op jit(solution)/shard_map/ppermute | solution.py:134
  116.6 6.4 %collective-permute-start.9 = (bf16[64,512]{1,0:T(8,128)(2,1)S(1)}, bf16[64,512]{1,0:T(8,128)(2,1)S(1)}, u32[]{:S(2)}, u32[]{:S(2)}) collective-permute-start(bf16[64,512]{1,0:T(8,128)(2,1)S(1)} %collective-permute-done.8), channel_id=1, source_target_pairs={{0,1},{1,2},{2,3},{3,4},{4,5},{5,6},{6,7},{7,8},{8,9},{9,10},{10,1... | collective-permute-start | bytes 196616 | tf_op jit(solution)/shard_map/ppermute | solution.py:134
  122.9 6.4 %collective-permute-start.10 = (bf16[64,512]{1,0:T(8,128)(2,1)S(1)}, bf16[64,512]{1,0:T(8,128)(2,1)S(1)}, u32[]{:S(2)}, u32[]{:S(2)}) collective-permute-start(bf16[64,512]{1,0:T(8,128)(2,1)S(1)} %collective-permute-done.9), channel_id=1, source_target_pairs={{0,1},{1,2},{2,3},{3,4},{4,5},{5,6},{6,7},{7,8},{8,9},{9,10},{10,1... | collective-permute-start | bytes 196616 | tf_op jit(solution)/shard_map/ppermute | solution.py:134
  129.3 6.4 %collective-permute-start.11 = (bf16[64,512]{1,0:T(8,128)(2,1)S(1)}, bf16[64,512]{1,0:T(8,128)(2,1)S(1)}, u32[]{:S(2)}, u32[]{:S(2)}) collective-permute-start(bf16[64,512]{1,0:T(8,128)(2,1)S(1)} %collective-permute-done.10), channel_id=1, source_target_pairs={{0,1},{1,2},{2,3},{3,4},{4,5},{5,6},{6,7},{7,8},{8,9},{9,10},{10,1... | collective-permute-start | bytes 196616 | tf_op jit(solution)/shard_map/ppermute | solution.py:134
  135.7 6.4 %collective-permute-start.12 = (bf16[64,512]{1,0:T(8,128)(2,1)S(1)}, bf16[64,512]{1,0:T(8,128)(2,1)S(1)}, u32[]{:S(2)}, u32[]{:S(2)}) collective-permute-start(bf16[64,512]{1,0:T(8,128)(2,1)S(1)} %collective-permute-done.11), channel_id=1, source_target_pairs={{0,1},{1,2},{2,3},{3,4},{4,5},{5,6},{6,7},{7,8},{8,9},{9,10},{10,1... | collective-permute-start | bytes 196616 | tf_op jit(solution)/shard_map/ppermute | solution.py:134
  142.1 6.6 %collective-permute-start.13 = (bf16[64,512]{1,0:T(8,128)(2,1)S(1)}, bf16[64,512]{1,0:T(8,128)(2,1)S(1)}, u32[]{:S(2)}, u32[]{:S(2)}) collective-permute-start(bf16[64,512]{1,0:T(8,128)(2,1)S(1)} %collective-permute-done.12), channel_id=1, source_target_pairs={{0,1},{1,2},{2,3},{3,4},{4,5},{5,6},{6,7},{7,8},{8,9},{9,10},{10,1... | collective-permute-start | bytes 196616 | tf_op jit(solution)/shard_map/ppermute | solution.py:134
  148.7 6.2 %collective-permute-start.14 = (bf16[64,512]{1,0:T(8,128)(2,1)S(1)}, bf16[64,512]{1,0:T(8,128)(2,1)S(1)}, u32[]{:S(2)}, u32[]{:S(2)}) collective-permute-start(bf16[64,512]{1,0:T(8,128)(2,1)S(1)} %collective-permute-done.13), channel_id=1, source_target_pairs={{0,1},{1,2},{2,3},{3,4},{4,5},{5,6},{6,7},{7,8},{8,9},{9,10},{10,1... | collective-permute-start | bytes 196616 | tf_op jit(solution)/shard_map/ppermute | solution.py:134
  205.1 1.2 copy-start.1
  205.2 1.5 copy-start.2
  206.7 1.2 copy-start.3
  223.0 1.2 copy-start.1
  223.0 1.5 copy-start.2
  224.6 1.2 copy-start.3
Sparse Core Ops, SparseCore 0:
  11.7 55.6 reduce-scatter.1
  153.8 46.5 all-gather.1
